TPU v7x, 1024 devices: a whole 4x4x32 slice. The times are simulated.
1024 devices in a mesh: dp: 8 (over x, core), chan: 4 (over z_hi), ctx: 32 (over y, z_lo).
Axes of the slice: x: 4, y: 4, z: 32 (z_hi: 4, z_lo: 8; z = z_hi * 8 + z_lo), core: 2. Of those that a mesh axis runs over, the one named last changes fastest.
Arguments:
- query_proj: bfloat16 [8, 4096, 4096], P('dp', 'ctx', 'chan'), may hold values from -6 to 6
- key_proj: bfloat16 [8, 4096, 4096], P('dp', 'ctx', 'chan'), may hold values from -6 to 6
- value_proj: bfloat16 [8, 4096, 4096], P('dp', 'ctx', 'chan'), may hold values from -6 to 6
- out_grad: bfloat16 [8, 4096, 4096], P('dp', 'ctx', 'chan'), may hold values from -6 to 6
- filter_taps: float32 [4096, 4096], P(('chan', 'ctx')), may hold values from -0.09375 to 0.09375
Outputs:
- grad_q: bfloat16 [8, 4096, 4096], P('dp', 'ctx', 'chan')
- grad_k: bfloat16 [8, 4096, 4096], P('dp', 'ctx', 'chan')
- grad_v: bfloat16 [8, 4096, 4096], P('dp', 'ctx', 'chan')
- grad_filt: float32 [4096, 4096], P(('chan', 'ctx'))
All inputs are finite; a program needn't handle non-finite values.
Results may differ from a plain program's by a relative error of at most 0.014.
Values may be sent and summed in bfloat16 or wider, within the bound.
A program may use at most 64 MiB of HBM per device.

v0:
```python
import math

import jax
import jax.numpy as jnp
from jax import lax
from jax.sharding import PartitionSpec as P

exact_mode = lax.Precision.HIGHEST
field_mode = lax.Precision.HIGH


def factor_sizes(length):
    col_count = min(128, length)
    return (2 * length // col_count, col_count)


def angle_table(first_size, second_size, period):
    product = (
        jnp.arange(first_size, dtype=jnp.int32)[:, None]
        * jnp.arange(second_size, dtype=jnp.int32)[None, :]
        % period
    )
    angles = product.astype(jnp.float32) * (2.0 * math.pi / period)
    return (jnp.cos(angles), jnp.sin(angles))


def make_tables(length):
    row_count, col_count = factor_sizes(length)
    outer_cos, outer_sin = angle_table(row_count, row_count // 2, row_count)
    twist_cos, twist_sin = angle_table(row_count, col_count, row_count * col_count)
    inner_cos, inner_sin = angle_table(col_count, col_count, col_count)
    real_outer = jnp.stack([outer_cos, -outer_sin])
    mixed_outer = jnp.stack([jnp.stack([outer_cos, outer_sin]), jnp.stack([-outer_sin, outer_cos])])
    fwd_twist = jnp.stack([twist_cos, -twist_sin])[:, None]
    inv_twist = jnp.stack([twist_cos, twist_sin])[:, None]
    fwd_inner = jnp.stack([jnp.stack([inner_cos, -inner_sin]), jnp.stack([inner_sin, inner_cos])])
    inv_inner = jnp.stack([jnp.stack([inner_cos, inner_sin]), jnp.stack([-inner_sin, inner_cos])])
    back_outer = jnp.stack([outer_cos, -outer_sin]) / float(row_count * col_count)
    return (real_outer, mixed_outer, fwd_twist, inv_twist, fwd_inner, inv_inner, back_outer)


def complex_mul(left, right):
    return jnp.stack(
        [left[0] * right[0] - left[1] * right[1], left[0] * right[1] + left[1] * right[0]]
    )


def conjugate(values):
    return jnp.stack([values[0], -values[1]])


def forward(values, tables, mode, is_pair):
    real_outer, mixed_outer, fwd_twist, inv_twist, fwd_inner, inv_inner, back_outer = tables
    half_rows = real_outer.shape[2]
    col_count = fwd_inner.shape[2]
    if is_pair:
        grid = values.reshape(2, values.shape[1], half_rows, col_count)
        first = jnp.einsum("stca,thab->shcb", mixed_outer, grid, precision=mode)
    else:
        grid = values.reshape(values.shape[0], half_rows, col_count)
        first = jnp.einsum("sca,hab->shcb", real_outer, grid, precision=mode)
    turned = complex_mul(first, fwd_twist)
    return jnp.einsum("shcb,stbd->thcd", turned, fwd_inner, precision=mode)


def inverse(spectrum, tables, mode):
    real_outer, mixed_outer, fwd_twist, inv_twist, fwd_inner, inv_inner, back_outer = tables
    back = jnp.einsum("shcd,stdb->thcb", spectrum, inv_inner, precision=mode)
    turned = complex_mul(back, inv_twist)
    out_grid = jnp.einsum("sca,shcb->hab", back_outer, turned, precision=mode)
    return out_grid.reshape(out_grid.shape[0], -1)


def split_packed(packed):
    rows_flipped = jnp.roll(jnp.flip(packed, axis=2), 1, axis=2)
    cols_flipped = jnp.flip(rows_flipped, axis=3)
    cols_rolled = jnp.roll(cols_flipped, 1, axis=3)
    first_row = (jnp.arange(packed.shape[2]) == 0)[None, None, :, None]
    mirrored = jnp.where(first_row, cols_rolled, cols_flipped)
    gate_spec = jnp.stack([0.5 * (packed[0] + mirrored[0]), 0.5 * (packed[1] - mirrored[1])])
    grad_spec = jnp.stack([0.5 * (packed[1] + mirrored[1]), 0.5 * (mirrored[0] - packed[0])])
    return (gate_spec, grad_spec)


def local(query_proj, key_proj, value_proj, out_grad, filter_taps):
    query_vals = query_proj[0].astype(jnp.float32)
    key_vals = key_proj[0].astype(jnp.float32)
    grad_vals = out_grad[0].astype(jnp.float32)
    gated_vals = (query_vals * key_vals).astype(jnp.bfloat16).T
    grad_conv = (grad_vals * value_proj[0].astype(jnp.float32)).astype(jnp.bfloat16).T
    length = filter_taps.shape[1]
    tables = make_tables(length)
    filt_spec = forward(filter_taps, tables, exact_mode, False)
    gated_all, grad_all = (
        lax.all_to_all(gated_vals, "ctx", split_axis=0, concat_axis=1, tiled=True),
        lax.all_to_all(grad_conv, "ctx", split_axis=0, concat_axis=1, tiled=True),
    )
    packed = forward(
        jnp.stack([gated_all.astype(jnp.float32), grad_all.astype(jnp.float32)]),
        tables,
        field_mode,
        True,
    )
    gate_spec, grad_spec = split_packed(packed)
    channel_count = gated_all.shape[0]
    joined = jnp.concatenate(
        [complex_mul(gate_spec, filt_spec), complex_mul(grad_spec, conjugate(filt_spec))], axis=1
    )
    results = inverse(joined, tables, field_mode).astype(jnp.bfloat16)
    conv_full = results[:channel_count]
    back_full = results[channel_count:]
    conv_local, back_local = (
        lax.all_to_all(conv_full, "ctx", split_axis=1, concat_axis=0, tiled=True),
        lax.all_to_all(back_full, "ctx", split_axis=1, concat_axis=0, tiled=True),
    )
    grad_v = (grad_vals * conv_local.T.astype(jnp.float32)).astype(jnp.bfloat16)[None]
    back_vals = back_local.T.astype(jnp.float32)
    grad_q = (back_vals * key_vals).astype(jnp.bfloat16)[None]
    grad_k = (back_vals * query_vals).astype(jnp.bfloat16)[None]
    cross_spec = complex_mul(conjugate(gate_spec), grad_spec)
    grad_filt = lax.psum(inverse(cross_spec, tables, exact_mode).astype(jnp.bfloat16), "dp").astype(
        jnp.float32
    )
    return (grad_q, grad_k, grad_v, grad_filt)


def solution(mesh):
    return jax.shard_map(
        local,
        mesh=mesh,
        in_specs=(
            P("dp", "ctx", "chan"),
            P("dp", "ctx", "chan"),
            P("dp", "ctx", "chan"),
            P("dp", "ctx", "chan"),
            P(("chan", "ctx"), None),
        ),
        out_specs=(
            P("dp", "ctx", "chan"),
            P("dp", "ctx", "chan"),
            P("dp", "ctx", "chan"),
            P(("chan", "ctx"), None),
        ),
        check_vma=False,
    )
```

profile of v0, /device:TPU:1, one launch (start us, length us, event | category | flops | bytes accessed | tf_op | source)
XLA Modules:
  0.0 251.4 jit_solution(14196545551190854167)
XLA Ops:
  7.2 1.2 copy.37
  8.4 1.2 copy.38
  9.6 0.8 fusion.47
  10.4 16.1 %all-to-all-start = ((bf16[32,32,128]{2,1,0:T(8,128)(2,1)}), bf16[32,32,128]{2,1,0:T(8,128)(2,1)S(1)}, u32[]{:S(2)}, u32[]{:S(2)}) async-start(bf16[32,32,128]{2,1,0:T(8,128)(2,1)} %bitcast.11), calls=%async_computation | async-start | bytes 524288 | tf_op jit(solution)/shard_map/all_to_all | solution.py:95
  26.9 0.8 fusion.45
  27.7 17.6 %all-to-all-done = bf16[32,32,128]{2,1,0:T(8,128)(2,1)S(1)} async-done(((bf16[32,32,128]{2,1,0:T(8,128)(2,1)}), bf16[32,32,128]{2,1,0:T(8,128)(2,1)S(1)}, u32[]{:S(2)}, u32[]{:S(2)}) %all-to-all-start) | async-done | bytes 262176 | tf_op jit(solution)/shard_map/all_to_all | solution.py:95
  45.2 5.1 %all-to-all-start.1 = ((bf16[32,32,128]{2,1,0:T(8,128)(2,1)}), bf16[32,32,128]{2,1,0:T(8,128)(2,1)S(1)}, u32[]{:S(2)}, u32[]{:S(2)}) async-start(bf16[32,32,128]{2,1,0:T(8,128)(2,1)} %bitcast.17), calls=%async_computation.1 | async-start | bytes 524288 | tf_op jit(solution)/shard_map/all_to_all | solution.py:96
  50.5 0.5 iota_compare_fusion
  51.2 0.8 fusion.87
  52.0 0.8 fusion.88
  53.0 0.6 fusion.67
  53.9 0.7 fusion.57
  54.6 0.8 pad_maximum_fusion.1
  55.4 1.8 convolution_bitcast_fusion
  57.4 11.7 %all-to-all-done.1 = bf16[32,32,128]{2,1,0:T(8,128)(2,1)S(1)} async-done(((bf16[32,32,128]{2,1,0:T(8,128)(2,1)}), bf16[32,32,128]{2,1,0:T(8,128)(2,1)S(1)}, u32[]{:S(2)}, u32[]{:S(2)}) %all-to-all-start.1) | async-done | bytes 262176 | tf_op jit(solution)/shard_map/all_to_all | solution.py:96
  69.2 1.5 convolution_bitcast_fusion.1
  70.7 2.6 %multiply_subtract_fusion.5 = (f32[1,32,64,128]{3,2,0,1:T(8,128)S(1)}, f32[1,32,64,128]{3,2,0,1:T(8,128)}, f32[1,32,64,128]{3,2,0,1:T(8,128)S(1)}, f32[1,32,64,128]{3,2,0,1:T(8,128)S(1)}) fusion(f32[2,32,64,128]{3,2,0,1:T(8,128)S(1)} %convolution_bitcast_fusion, f32[64,128]{1,0:T(8,128)} %get-tuple-element.51, f32[64,128]{1,0:T(8,128)} %get-tuple-element.50, ...), kind=kLoop, calls=%fused_computation.54 | loop fusion | flops 3145728 | bytes 8454144 | tf_op jit(solution)/shard_map/sub | solution.py:44
  73.4 1.0 fusion.25
  74.4 1.8 slice.136
  76.3 0.6 slice.135
  77.0 2.6 %slice.115 = f32[2,32,63,128]{3,2,1,0:T(8,128)S(1)} reverse(f32[2,32,63,128]{3,2,1,0:T(8,128)} %slice.136), dimensions={2} | reverse | bytes 4128768 | tf_op jit(solution)/shard_map/jit(_roll_static)/slice | solution.py:75
  79.6 2.5 fusion.10
  82.1 2.1 fusion.11
  84.1 1.7 pad_maximum_fusion
  85.8 4.3 %slice.118 = f32[2,32,64,127]{3,2,1,0:T(8,128)} reverse(f32[2,32,64,127]{3,2,1,0:T(8,128)} %fusion.11), dimensions={3} | reverse | bytes 4161536 | tf_op jit(solution)/shard_map/jit(_roll_static)/slice | solution.py:77
  90.1 2.4 rev.6
  92.5 3.8 %maximum_select_fusion = f32[2,32,64,128]{3,2,1,0:T(8,128)S(1)} fusion(f32[2,32,64,128]{3,2,1,0:T(8,128)} %rev.6, f32[2,32,64,127]{3,2,1,0:T(8,128)} %slice.118, f32[2,32,64,1]{3,2,1,0:T(8,128)} %fusion.10, pred[64]{0:T(512)(128)(4,1)} %iota_compare_fusion), kind=kLoop, calls=%fused_computation.18 | loop fusion | flops 1048576 | bytes 6291520 | tf_op jit(solution)/shard_map/jit(_where)/select_n | solution.py:79
  96.3 0.6 multiply_subtract_fusion.2
  96.9 0.6 copy-done.3
  97.5 1.9 fusion.24
  99.5 1.1 multiply_subtract_fusion.4
  100.6 2.0 fusion.7
  102.6 1.0 multiply_subtract_fusion
  103.6 1.2 fusion.35
  104.9 0.7 fusion.106
  105.6 0.8 copy.46
  106.4 5.1 %all-to-all-start.2 = ((bf16[32,32,128]{2,0,1:T(8,128)(2,1)}), bf16[32,32,128]{2,0,1:T(8,128)(2,1)S(1)}, u32[]{:S(2)}, u32[]{:S(2)}) async-start(bf16[32,32,128]{2,0,1:T(8,128)(2,1)} %copy.46), calls=%async_computation.2 | async-start | bytes 524288 | tf_op jit(solution)/shard_map/all_to_all | solution.py:114
  111.5 1.8 copy.47
  113.3 17.0 %all-to-all-done.2 = bf16[32,32,128]{2,0,1:T(8,128)(2,1)S(1)} async-done(((bf16[32,32,128]{2,0,1:T(8,128)(2,1)}), bf16[32,32,128]{2,0,1:T(8,128)(2,1)S(1)}, u32[]{:S(2)}, u32[]{:S(2)}) %all-to-all-start.2) | async-done | bytes 262176 | tf_op jit(solution)/shard_map/all_to_all | solution.py:114
  130.3 5.1 %all-to-all-start.3 = ((bf16[32,32,128]{2,0,1:T(8,128)(2,1)}), bf16[32,32,128]{2,0,1:T(8,128)(2,1)S(1)}, u32[]{:S(2)}, u32[]{:S(2)}) async-start(bf16[32,32,128]{2,0,1:T(8,128)(2,1)} %copy.47), calls=%async_computation.3 | async-start | bytes 524288 | tf_op jit(solution)/shard_map/all_to_all | solution.py:113
  135.7 1.9 fusion.26
  138.1 1.3 fusion.41
  139.4 0.8 copy.93
  140.2 99.8 %all-reduce.2.cloned.1.call-done = bf16[32,4096]{1,0:T(8,128)(2,1)} async-done(((bf16[32,4096]{1,0:T(8,128)(2,1)}), bf16[32,4096]{1,0:T(8,128)(2,1)}) %all-reduce.2.cloned.1.call-update) | async-done | bytes 262160 | tf_op jit(solution)/shard_map/psum | solution.py:121
  240.0 1.8 convert_element_type.236
  241.9 0.9 copy.51
  242.8 0.8 copy.52
  243.7 0.9 copy.53
  (54 shorter events, 2.5 us)
Async XLA Ops:
  7.2 19.3 %copy-start.18 = (bf16[1,128,1024]{2,1,0:T(8,128)(2,1)S(1)}, bf16[1,128,1024]{2,1,0:T(8,128)(2,1)}, u32[]{:S(2)}) copy-start(bf16[1,128,1024]{2,1,0:T(8,128)(2,1)} %param.8) | copy-start | bytes 786436
  7.2 19.5 %copy-start.19 = (bf16[1,128,1024]{2,1,0:T(8,128)(2,1)S(1)}, bf16[1,128,1024]{2,1,0:T(8,128)(2,1)}, u32[]{:S(2)}) copy-start(bf16[1,128,1024]{2,1,0:T(8,128)(2,1)} %param.7) | copy-start | bytes 786436
  8.4 36.9 %copy-start.4 = (bf16[1,128,1024]{1,2,0:T(8,128)(2,1)}, bf16[1,128,1024]{1,2,0:T(8,128)(2,1)S(1)}, u32[]{:S(2)}) copy-start(bf16[1,128,1024]{1,2,0:T(8,128)(2,1)S(1)} %copy.37) | copy-start | bytes 786436
  8.4 42.0 %copy-start.13 = (f32[32,4096]{1,0:T(8,128)S(1)}, f32[32,4096]{1,0:T(8,128)}, u32[]{:S(2)}) copy-start(f32[32,4096]{1,0:T(8,128)} %param.9) | copy-start | bytes 1572868
  9.6 40.9 %copy-start.6 = (bf16[1,128,1024]{1,2,0:T(8,128)(2,1)}, bf16[1,128,1024]{1,2,0:T(8,128)(2,1)S(1)}, u32[]{:S(2)}) copy-start(bf16[1,128,1024]{1,2,0:T(8,128)(2,1)S(1)} %copy.38) | copy-start | bytes 786436
  10.4 34.8 %all-to-all-start = ((bf16[32,32,128]{2,1,0:T(8,128)(2,1)}), bf16[32,32,128]{2,1,0:T(8,128)(2,1)S(1)}, u32[]{:S(2)}, u32[]{:S(2)}) async-start(bf16[32,32,128]{2,1,0:T(8,128)(2,1)} %bitcast.11), calls=%async_computation | async-start | bytes 524288 | tf_op jit(solution)/shard_map/all_to_all | solution.py:95
  45.2 23.9 %all-to-all-start.1 = ((bf16[32,32,128]{2,1,0:T(8,128)(2,1)}), bf16[32,32,128]{2,1,0:T(8,128)(2,1)S(1)}, u32[]{:S(2)}, u32[]{:S(2)}) async-start(bf16[32,32,128]{2,1,0:T(8,128)(2,1)} %bitcast.17), calls=%async_computation.1 | async-start | bytes 524288 | tf_op jit(solution)/shard_map/all_to_all | solution.py:96
  51.2 6.1 %copy-start.14 = (f32[1,64,32]{1,2,0:T(8,128)}, f32[1,64,32]{1,2,0:T(8,128)S(1)}, u32[]{:S(2)}) copy-start(f32[1,64,32]{1,2,0:T(8,128)S(1)} %get-tuple-element.49) | copy-start | bytes 24580
  70.7 2.6 %copy-start.8 = (f32[1,2,128,128]{3,2,0,1:T(8,128)S(1)}, f32[1,2,128,128]{3,2,0,1:T(8,128)}, u32[]{:S(2)}) copy-start(f32[1,2,128,128]{3,2,0,1:T(8,128)} %get-tuple-element.42) | copy-start | bytes 393220
  74.4 2.0 copy-start
  79.6 2.5 copy-start.12
  85.8 4.3 %copy-start.2 = (f32[2,32,64,128]{3,2,1,0:T(8,128)S(1)}, f32[2,32,64,128]{3,2,1,0:T(8,128)}, u32[]{:S(2)}) copy-start(f32[2,32,64,128]{3,2,1,0:T(8,128)} %pad_maximum_fusion) | copy-start | bytes 6291460
  92.5 3.8 %copy-start.1 = (f32[2,32,64,128]{3,2,1,0:T(8,128)S(1)}, f32[2,32,64,128]{3,2,1,0:T(8,128)}, u32[]{:S(2)}) copy-start(f32[2,32,64,128]{3,2,1,0:T(8,128)} %copy-done) | copy-start | bytes 6291460
  96.3 1.2 copy-start.3
  96.3 1.2 copy-start.9
  99.5 1.1 copy-start.17
  100.6 2.0 copy-start.11
  100.6 2.0 copy-start.16
  102.6 1.0 copy-start.15
  104.9 30.8 %copy-start.10 = (f32[2,2,128,128]{3,2,1,0:T(8,128)S(1)}, f32[2,2,128,128]{3,2,1,0:T(8,128)}, u32[]{:S(2)}) copy-start(f32[2,2,128,128]{3,2,1,0:T(8,128)} %get-tuple-element.34) | copy-start | bytes 786436
  106.4 23.8 %all-to-all-start.2 = ((bf16[32,32,128]{2,0,1:T(8,128)(2,1)}), bf16[32,32,128]{2,0,1:T(8,128)(2,1)S(1)}, u32[]{:S(2)}, u32[]{:S(2)}) async-start(bf16[32,32,128]{2,0,1:T(8,128)(2,1)} %copy.46), calls=%async_computation.2 | async-start | bytes 524288 | tf_op jit(solution)/shard_map/all_to_all | solution.py:114
  130.3 113.4 %all-to-all-start.3 = ((bf16[32,32,128]{2,0,1:T(8,128)(2,1)}), bf16[32,32,128]{2,0,1:T(8,128)(2,1)S(1)}, u32[]{:S(2)}, u32[]{:S(2)}) async-start(bf16[32,32,128]{2,0,1:T(8,128)(2,1)} %copy.47), calls=%async_computation.3 | async-start | bytes 524288 | tf_op jit(solution)/shard_map/all_to_all | solution.py:113
  135.4 104.6 %all-reduce.2.cloned.1.call-start = ((), (), s32[]{:S(2)}) async-start(), calls=%async_computation.4 | async-start | bytes 524288 | tf_op jit(solution)/shard_map/psum | solution.py:121
  138.0 103.8 %copy-start.5 = (bf16[1,128,1024]{1,2,0:T(8,128)(2,1)S(1)}, bf16[1,128,1024]{1,2,0:T(8,128)(2,1)}, u32[]{:S(2)}) copy-start(bf16[1,128,1024]{1,2,0:T(8,128)(2,1)} %copy-done.4) | copy-start | bytes 786436
  138.0 103.7 %copy-start.7 = (bf16[1,128,1024]{1,2,0:T(8,128)(2,1)S(1)}, bf16[1,128,1024]{1,2,0:T(8,128)(2,1)}, u32[]{:S(2)}) copy-start(bf16[1,128,1024]{1,2,0:T(8,128)(2,1)} %copy-done.6) | copy-start | bytes 786436
Sparse Core Ops, SparseCore 0:
  140.3 99.6 all-reduce.1
where the time goes:
time: 252 us; the launch traced here: 251 us
  waiting for transfers between devices  146 us (58%)
  starting transfers between devices  31.7 us (13%)
  other arithmetic  24.2 us (10%)
  local copies, waits for them, and re-layouts  22.2 us (9%)
  between operations  14.5 us (6%)
  matrix products  12.7 us (5%)
    psum x1, waiting for transfers between devices, local(): lax.psum(inverse(cross_spec, tables, exact_mode).astype(jnp.bfloat16), 'dp')  99.8 us
    all_to_all x1, waiting for transfers between devices, local(): lax.all_to_all(gated_vals, 'ctx', split_axis=0, concat_axis=1, tiled=True)  17.6 us
    all_to_all x1, waiting for transfers between devices, local(): lax.all_to_all(back_full, 'ctx', split_axis=1, concat_axis=0, tiled=True)  17 us
    all_to_all x1, starting transfers between devices, local(): lax.all_to_all(gated_vals, 'ctx', split_axis=0, concat_axis=1, tiled=True)  16.1 us
    all_to_all x1, waiting for transfers between devices, local(): lax.all_to_all(grad_conv, 'ctx', split_axis=0, concat_axis=1, tiled=True)  11.7 us
    unnamed x49, local copies, waits for them, and re-layouts  7.04 us
    concatenate x3, other arithmetic, split_packed(): rows_flipped = jnp.roll(jnp.flip(packed, axis=2), 1, axis=2)  6.26 us
    sub x5, other arithmetic, complex_mul(): left[0] * right[0] - left[1] * right[1]  5.69 us
  transfers between devices with their start and end apart: 5, of which 4 were waited for; matrix products, arithmetic and copies ran while one was open for 7% of the time, Pallas kernels for 0%

commit v1 on v0

v1 whole, which is shorter than its diff:
```python
import functools
import math

import jax
import jax.numpy as jnp
import ml_dtypes
import numpy as np
from jax import lax
from jax.experimental import pallas as pl
from jax.experimental.pallas import tpu as pltpu
from jax.sharding import PartitionSpec as P

MESH = pl.DeviceIdType.MESH
ROWS = 16
COLS = 128
F32 = jnp.float32
BF16 = jnp.bfloat16


def make_tables(blocks):
    freq = np.arange(blocks) + 0.5
    outer = np.exp(-2j * np.pi * np.outer(freq, np.arange(blocks)) / (2 * blocks))
    eye = np.eye(ROWS)
    spread = lambda table: np.kron(table, eye)
    outer_fwd = np.concatenate([spread(outer.real), spread(outer.imag)], axis=0)
    length = 2 * blocks * COLS
    back = outer.conj().T * (2.0 / length)
    outer_inv = np.concatenate([spread(back.real), spread(-back.imag)], axis=1)
    inner = np.exp(-2j * np.pi * np.outer(np.arange(COLS), np.arange(COLS)) / COLS)
    inner_fwd = np.block([[inner.real, inner.imag], [-inner.imag, inner.real]])
    inner_inv = np.block([[inner.real, -inner.imag], [inner.imag, inner.real]])
    twist = np.exp(-2j * np.pi * np.outer(freq, np.arange(COLS)) / length)
    twist = np.repeat(twist, ROWS, axis=0)
    half = lambda table: np.asarray(table).astype(ml_dtypes.bfloat16)
    full = lambda table: np.asarray(table).astype(np.float32)
    return (half(outer_fwd), half(outer_inv), half(inner_fwd), half(inner_inv), full(twist.real), full(twist.imag))


def dot(left, right):
    return jnp.dot(left, right, preferred_element_type=F32)


def kernel(
    blocks, parts, cols,
    query_ref, key_ref, value_ref, grad_ref, taps_ref,
    outer_fwd, outer_inv, inner_fwd, inner_inv, twist_re, twist_im,
    conv_out, back_out, filt_out,
    send_buf, recv_buf, ret_send, ret_recv,
    filt_re, filt_im, cross_rows, cross_buf, part_buf, sum_buf, full_buf,
    send_sem, recv_sem, ret_send_sem, ret_recv_sem, own_sem, red_send, red_recv, all_send, all_recv,
):
    me = lax.axis_index("ctx")
    mine = lax.axis_index("dp")
    lines = blocks // cols
    row_at, col_at = me // cols, me % cols
    span = blocks * ROWS
    group = COLS // (2 * ROWS)
    piece = blocks // parts

    def peer(step):
        turn = step // lines
        shift = cols // 2 + ((turn + 1) // 2) * (1 - 2 * (turn % 2))
        down = (step % lines + 1) % lines
        return ((row_at + down) % lines) * cols + (col_at + shift) % cols

    barrier = pltpu.get_barrier_semaphore()

    def greet(step, carry):
        pl.semaphore_signal(barrier, inc=1, device_id={"ctx": peer(step)}, device_id_type=MESH)
        return carry

    def greet_part(step, carry):
        pl.semaphore_signal(barrier, inc=1, device_id={"dp": (mine + 1 + step) % parts}, device_id_type=MESH)
        return carry

    lax.fori_loop(0, blocks - 1, greet, 0)
    lax.fori_loop(0, parts - 1, greet_part, 0)

    for number, (left_ref, right_ref) in enumerate(((query_ref, key_ref), (grad_ref, value_ref))):
        for block in range(blocks // group):
            lanes = slice(block * COLS, (block + 1) * COLS)
            product = left_ref[:, lanes].astype(F32) * right_ref[:, lanes].astype(F32)
            turned = product.T.astype(BF16).reshape(group, 2, ROWS, COLS)
            for half in range(2):
                send_buf[half, number, block * group:(block + 1) * group] = turned[:, half]

    pl.semaphore_wait(barrier, blocks - 1 + parts - 1)

    def send_tokens(half):
        def start(step, carry):
            dest = peer(step)
            pltpu.make_async_remote_copy(
                src_ref=send_buf.at[half, :, dest], dst_ref=recv_buf.at[half, :, me],
                send_sem=send_sem.at[half], recv_sem=recv_sem.at[half],
                device_id={"ctx": dest}, device_id_type=MESH,
            ).start()
            return carry

        lax.fori_loop(0, blocks - 1, start, 0)

    def send_back(half):
        def start(step, carry):
            dest = peer(step)
            pltpu.make_async_remote_copy(
                src_ref=ret_send.at[half, :, dest], dst_ref=ret_recv.at[half, :, me],
                send_sem=ret_send_sem.at[half], recv_sem=ret_recv_sem.at[half],
                device_id={"ctx": dest}, device_id_type=MESH,
            ).start()
            return carry

        lax.fori_loop(0, blocks - 1, start, 0)

    def wait_bytes(ref, sem):
        pltpu.make_async_copy(ref, ref, sem).wait()

    def others(ref, half):
        return ref.at[half, :, pl.ds(0, blocks - 1)]

    def own_copy(half):
        return pltpu.make_async_copy(send_buf.at[half, :, me], recv_buf.at[half, :, me], own_sem.at[half])

    def own_back(half):
        return pltpu.make_async_copy(ret_send.at[half, :, me], ret_recv.at[half, :, me], own_sem.at[2 + half])

    for half in range(2):
        send_tokens(half)
    for half in range(2):
        own_copy(half).start()

    def forward(rows):
        first = dot(outer_fwd[...], rows)
        spectra = []
        for block in range(2):
            lanes = slice(block * COLS, (block + 1) * COLS)
            real, imag = first[:span, lanes], first[span:, lanes]
            turned_re = real * twist_re[...] - imag * twist_im[...]
            turned_im = real * twist_im[...] + imag * twist_re[...]
            both = jnp.concatenate([turned_re.astype(BF16), turned_im.astype(BF16)], axis=1)
            result = dot(both, inner_fwd[...])
            spectra.append((result[:, :COLS], result[:, COLS:]))
        return spectra

    def inverse_inner(real, imag):
        both = jnp.concatenate([real.astype(BF16), imag.astype(BF16)], axis=1)
        result = dot(both, inner_inv[...])
        real, imag = result[:, :COLS], result[:, COLS:]
        turned_re = real * twist_re[...] + imag * twist_im[...]
        turned_im = imag * twist_re[...] - real * twist_im[...]
        return jnp.concatenate([turned_re.astype(BF16), turned_im.astype(BF16)], axis=0)

    taps_rows = jnp.concatenate(
        [
            jnp.concatenate(
                [taps_ref[half * ROWS:(half + 1) * ROWS, a * COLS:(a + 1) * COLS] for a in range(blocks)], axis=0
            ).astype(BF16)
            for half in range(2)
        ],
        axis=1,
    )
    for half, (real, imag) in enumerate(forward(taps_rows)):
        filt_re[half] = real
        filt_im[half] = imag

    for half in range(2):
        wait_bytes(others(recv_buf, half), recv_sem.at[half])
        own_copy(half).wait()
        rows = jnp.concatenate(
            [recv_buf[half, 0].reshape(span, COLS), recv_buf[half, 1].reshape(span, COLS)], axis=1
        )
        (gate_re, gate_im), (grad_re, grad_im) = forward(rows)
        tap_re, tap_im = filt_re[half], filt_im[half]
        conv = inverse_inner(gate_re * tap_re - gate_im * tap_im, gate_re * tap_im + gate_im * tap_re)
        back = inverse_inner(grad_re * tap_re + grad_im * tap_im, grad_im * tap_re - grad_re * tap_im)
        result = dot(outer_inv[...], jnp.concatenate([conv, back], axis=1)).astype(BF16)
        ret_send[half, 0] = result[:, :COLS].reshape(blocks, ROWS, COLS)
        ret_send[half, 1] = result[:, COLS:].reshape(blocks, ROWS, COLS)
        send_back(half)
        own_back(half).start()
        cross_rows[half] = inverse_inner(gate_re * grad_re + gate_im * grad_im, gate_re * grad_im - gate_im * grad_re)

    cross = dot(outer_inv[...], jnp.concatenate([cross_rows[0], cross_rows[1]], axis=1)).astype(BF16)
    for half in range(2):
        cross_buf[:, half * ROWS:(half + 1) * ROWS] = cross[:, half * COLS:(half + 1) * COLS].reshape(blocks, ROWS, COLS)

    def start_part(step, carry):
        dest = (mine + 1 + step) % parts
        pltpu.make_async_remote_copy(
            src_ref=cross_buf.at[pl.ds(dest * piece, piece)], dst_ref=part_buf.at[mine],
            send_sem=red_send.at[0], recv_sem=red_recv.at[0], device_id={"dp": dest}, device_id_type=MESH,
        ).start()
        return carry

    lax.fori_loop(0, parts - 1, start_part, 0)
    own_part = pltpu.make_async_copy(cross_buf.at[pl.ds(mine * piece, piece)], part_buf.at[mine], own_sem.at[4])
    own_part.start()
    wait_bytes(part_buf.at[pl.ds(0, parts - 1)], red_recv.at[0])
    own_part.wait()
    total = part_buf[0].astype(F32)
    for part in range(1, parts):
        total = total + part_buf[part].astype(F32)
    sum_buf[...] = total.astype(BF16)

    def start_sum(step, carry):
        dest = (mine + 1 + step) % parts
        pltpu.make_async_remote_copy(
            src_ref=sum_buf, dst_ref=full_buf.at[mine],
            send_sem=all_send.at[0], recv_sem=all_recv.at[0], device_id={"dp": dest}, device_id_type=MESH,
        ).start()
        return carry

    lax.fori_loop(0, parts - 1, start_sum, 0)
    own_sum = pltpu.make_async_copy(sum_buf, full_buf.at[mine], own_sem.at[5])
    own_sum.start()
    wait_bytes(full_buf.at[pl.ds(0, parts - 1)], all_recv.at[0])
    own_sum.wait()
    for a in range(blocks):
        filt_out[:, a * COLS:(a + 1) * COLS] = full_buf[a // piece, a % piece].astype(filt_out.dtype)

    for half in range(2):
        wait_bytes(others(ret_recv, half), ret_recv_sem.at[half])
        own_back(half).wait()
    for number, out_ref in enumerate((conv_out, back_out)):
        for block in range(blocks // group):
            owners = slice(block * group, (block + 1) * group)
            rows = jnp.stack([ret_recv[0, number, owners], ret_recv[1, number, owners]], axis=1)
            out_ref[:, block * COLS:(block + 1) * COLS] = rows.reshape(COLS, COLS).astype(F32).T.astype(BF16)

    for half in range(2):
        wait_bytes(others(send_buf, half), send_sem.at[half])
        wait_bytes(others(ret_send, half), ret_send_sem.at[half])
    wait_bytes(part_buf.at[pl.ds(0, parts - 1)], red_send.at[0])
    wait_bytes(full_buf.at[pl.ds(0, parts - 1)], all_send.at[0])


def local(blocks, parts, cols, query_proj, key_proj, value_proj, out_grad, filter_taps):
    tokens, channels = query_proj.shape[1:]
    tables = make_tables(blocks)
    span = blocks * ROWS
    piece = blocks // parts
    messages = (2, 2, blocks, ROWS, COLS)
    vmem = pl.BlockSpec(memory_space=pltpu.VMEM)
    conv_local, back_local, filt_sum = pl.pallas_call(
        functools.partial(kernel, blocks, parts, cols),
        out_shape=(
            jax.ShapeDtypeStruct((tokens, channels), BF16),
            jax.ShapeDtypeStruct((tokens, channels), BF16),
            jax.ShapeDtypeStruct(filter_taps.shape, BF16),
        ),
        in_specs=[vmem] * 11,
        out_specs=(vmem,) * 3,
        scratch_shapes=[
            pltpu.VMEM(messages, BF16),
            pltpu.VMEM(messages, BF16),
            pltpu.VMEM(messages, BF16),
            pltpu.VMEM(messages, BF16),
            pltpu.VMEM((2, span, COLS), F32),
            pltpu.VMEM((2, span, COLS), F32),
            pltpu.VMEM((2, 2 * span, COLS), BF16),
            pltpu.VMEM((blocks, 2 * ROWS, COLS), BF16),
            pltpu.VMEM((parts, piece, 2 * ROWS, COLS), BF16),
            pltpu.VMEM((piece, 2 * ROWS, COLS), BF16),
            pltpu.VMEM((parts, piece, 2 * ROWS, COLS), BF16),
            pltpu.SemaphoreType.DMA((2,)),
            pltpu.SemaphoreType.DMA((2,)),
            pltpu.SemaphoreType.DMA((2,)),
            pltpu.SemaphoreType.DMA((2,)),
            pltpu.SemaphoreType.DMA((6,)),
            pltpu.SemaphoreType.DMA((1,)),
            pltpu.SemaphoreType.DMA((1,)),
            pltpu.SemaphoreType.DMA((1,)),
            pltpu.SemaphoreType.DMA((1,)),
        ],
        compiler_params=pltpu.CompilerParams(
            collective_id=0, has_side_effects=True, vmem_limit_bytes=56 * 2**20
        ),
    )(query_proj[0], key_proj[0], value_proj[0], out_grad[0], filter_taps, *map(jnp.asarray, tables))
    back_vals = back_local.astype(F32)
    grad_q = (back_vals * key_proj[0].astype(F32)).astype(BF16)[None]
    grad_k = (back_vals * query_proj[0].astype(F32)).astype(BF16)[None]
    grad_v = (out_grad[0].astype(F32) * conv_local.astype(F32)).astype(BF16)[None]
    return grad_q, grad_k, grad_v, filt_sum.astype(F32)


def solution(mesh):
    blocks, parts = mesh.shape["ctx"], mesh.shape["dp"]
    cols = max(blocks // 4, 1)
    tokens = P("dp", "ctx", "chan")
    filt = P(("chan", "ctx"), None)
    return jax.shard_map(
        functools.partial(local, blocks, parts, cols),
        mesh=mesh,
        in_specs=(tokens, tokens, tokens, tokens, filt),
        out_specs=(tokens, tokens, tokens, filt),
        check_vma=False,
    )
```

time: 252 us -> 71.1 us (0.28)
  the two profiles are of different devices: /device:TPU:1 before, /device:TPU:353 now
where the time goes in v1:
time: 71.1 us; the launch traced here: 70.9 us
  Pallas kernels  67.3 us (95%)
  other arithmetic  2.96 us (4%)
    pallas_call x1, Pallas kernels, local(): pl.pallas_call(functools.partial(kernel, blocks, parts, cols), out_shape=...  67.3 us
    broadcast_in_dim x1, other arithmetic, local(): grad_k = (back_vals * query_proj[0].astype(F32)).astype(BF16)[None]  2.13 us

profile of v1, /device:TPU:353, one launch (start us, length us, event | category | flops | bytes accessed | tf_op | source)
XLA Modules:
  0.0 70.9 jit_solution(10479745557839001125)
XLA Ops:
  0.6 0.0 copy-start
  0.6 0.0 copy-start.1
  0.7 0.0 copy-start.2
  0.7 67.3 %shard_map.138 = (bf16[128,1024]{1,0:T(8,128)(2,1)}, bf16[128,1024]{1,0:T(8,128)(2,1)}, bf16[32,4096]{1,0:T(8,128)(2,1)}) custom-call(bf16[128,1024]{1,0:T(8,128)(2,1)} %bitcast.13, bf16[128,1024]{1,0:T(8,128)(2,1)} %bitcast.14, bf16[128,1024]{1,0:T(8,128)(2,1)} %bitcast.16, bf16[128,1024]{1,0:T(8,128)(2,1)} %bitcast.15, f32[32,4096]{1,0:T(8,128)} %taps_ref.1, ...), custom_call_target="tpu_custom_call" | custom-call | tf_op jit(solution)/shard_map/pallas_call | solution.py:242
  67.9 0.0 copy-done
  67.9 0.0 copy-done.1
  68.0 0.0 copy-done.2
  68.0 0.0 copy-start.3
  68.0 2.1 %fusion.3 = (bf16[1,128,1024]{2,1,0:T(8,128)(2,1)}, bf16[1,128,1024]{2,1,0:T(8,128)(2,1)}, bf16[1,128,1024]{2,1,0:T(8,128)(2,1)}) fusion(bf16[128,1024]{1,0:T(8,128)(2,1)} %get-tuple-element.7, bf16[1,128,1024]{2,1,0:T(8,128)(2,1)S(1)} %copy-done, bf16[1,128,1024]{2,1,0:T(8,128)(2,1)S(1)} %copy-done.1, bf16[128,1024]{1,0:T(8,128)(2,1)} %get-tuple-element.8, ...), kind=kLoop, calls=%fused_computation.6 | loop fusion | flops 1441792 | bytes 2097152 | tf_op jit(solution)/shard_map/broadcast_in_dim | solution.py:279
  70.1 0.0 copy-done.3
  70.1 0.8 %convert_element_type.35 = f32[32,4096]{1,0:T(8,128)} convert(bf16[32,4096]{1,0:T(8,128)(2,1)S(1)} %copy-done.3) | non-fusion elementwise | flops 131072 | bytes 786432 | tf_op jit(solution)/shard_map/convert_element_type | solution.py:281
Async XLA Ops:
  0.6 67.3 %copy-start = (bf16[1,128,1024]{2,1,0:T(8,128)(2,1)S(1)}, bf16[1,128,1024]{2,1,0:T(8,128)(2,1)}, u32[]{:S(2)}) copy-start(bf16[1,128,1024]{2,1,0:T(8,128)(2,1)} %param.11) | copy-start | bytes 786436
  0.6 67.3 %copy-start.1 = (bf16[1,128,1024]{2,1,0:T(8,128)(2,1)S(1)}, bf16[1,128,1024]{2,1,0:T(8,128)(2,1)}, u32[]{:S(2)}) copy-start(bf16[1,128,1024]{2,1,0:T(8,128)(2,1)} %param.12) | copy-start | bytes 786436
  0.7 67.3 %copy-start.2 = (bf16[1,128,1024]{2,1,0:T(8,128)(2,1)S(1)}, bf16[1,128,1024]{2,1,0:T(8,128)(2,1)}, u32[]{:S(2)}) copy-start(bf16[1,128,1024]{2,1,0:T(8,128)(2,1)} %param.14) | copy-start | bytes 786436
  68.0 2.1 %copy-start.3 = (bf16[32,4096]{1,0:T(8,128)(2,1)S(1)}, bf16[32,4096]{1,0:T(8,128)(2,1)}, u32[]{:S(2)}) copy-start(bf16[32,4096]{1,0:T(8,128)(2,1)} %get-tuple-element.9) | copy-start | bytes 786436

commit v2 on v1

--- a/solution.py
+++ b/solution.py
@@ -42,12 +42,14 @@
 
 def kernel(
     blocks, parts, cols,
+    query_hbm, key_hbm, value_hbm, grad_hbm, taps_hbm,
+    outer_fwd_hbm, outer_inv_hbm, inner_fwd_hbm, inner_inv_hbm, twist_re_hbm, twist_im_hbm,
+    conv_out, back_out, filt_out,
     query_ref, key_ref, value_ref, grad_ref, taps_ref,
     outer_fwd, outer_inv, inner_fwd, inner_inv, twist_re, twist_im,
-    conv_out, back_out, filt_out,
     send_buf, recv_buf, ret_send, ret_recv,
-    filt_re, filt_im, cross_rows, cross_buf, part_buf, sum_buf, full_buf,
-    send_sem, recv_sem, ret_send_sem, ret_recv_sem, own_sem, red_send, red_recv, all_send, all_recv,
+    filt_re, filt_im, cross_buf, part_buf, sum_buf, full_buf,
+    send_sem, recv_sem, ret_send_sem, ret_recv_sem, own_sem, load_sem, red_send, red_recv, all_send, all_recv,
 ):
     me = lax.axis_index("ctx")
     mine = lax.axis_index("dp")
@@ -76,7 +78,22 @@
     lax.fori_loop(0, blocks - 1, greet, 0)
     lax.fori_loop(0, parts - 1, greet_part, 0)
 
+    loads = [
+        pltpu.make_async_copy(source, target, load_sem.at[number])
+        for number, (source, target) in enumerate(
+            (
+                (query_hbm, query_ref), (key_hbm, key_ref), (grad_hbm, grad_ref), (value_hbm, value_ref),
+                (taps_hbm, taps_ref), (outer_fwd_hbm, outer_fwd), (inner_fwd_hbm, inner_fwd),
+                (twist_re_hbm, twist_re), (twist_im_hbm, twist_im),
+                (outer_inv_hbm, outer_inv), (inner_inv_hbm, inner_inv),
+            )
+        )
+    ]
+    for load in loads:
+        load.start()
     for number, (left_ref, right_ref) in enumerate(((query_ref, key_ref), (grad_ref, value_ref))):
+        loads[2 * number].wait()
+        loads[2 * number + 1].wait()
         for block in range(blocks // group):
             lanes = slice(block * COLS, (block + 1) * COLS)
             product = left_ref[:, lanes].astype(F32) * right_ref[:, lanes].astype(F32)
@@ -148,6 +165,8 @@
         turned_im = imag * twist_re[...] - real * twist_im[...]
         return jnp.concatenate([turned_re.astype(BF16), turned_im.astype(BF16)], axis=0)
 
+    for load in loads[4:]:
+        load.wait()
     taps_rows = jnp.concatenate(
         [
             jnp.concatenate(
@@ -161,7 +180,49 @@
         filt_re[half] = real
         filt_im[half] = imag
 
-    for half in range(2):
+    def start_part(half):
+        def start(step, carry):
+            dest = (mine + 1 + step) % parts
+            pltpu.make_async_remote_copy(
+                src_ref=cross_buf.at[half, pl.ds(dest * piece, piece)], dst_ref=part_buf.at[half, mine],
+                send_sem=red_send.at[half], recv_sem=red_recv.at[half], device_id={"dp": dest}, device_id_type=MESH,
+            ).start()
+            return carry
+
+        lax.fori_loop(0, parts - 1, start, 0)
+
+    def own_part(half):
+        return pltpu.make_async_copy(
+            cross_buf.at[half, pl.ds(mine * piece, piece)], part_buf.at[half, mine], own_sem.at[4 + half]
+        )
+
+    def start_sum(half):
+        def start(step, carry):
+            dest = (mine + 1 + step) % parts
+            pltpu.make_async_remote_copy(
+                src_ref=sum_buf.at[half], dst_ref=full_buf.at[half, mine],
+                send_sem=all_send.at[half], recv_sem=all_recv.at[half], device_id={"dp": dest}, device_id_type=MESH,
+            ).start()
+            return carry
+
+        lax.fori_loop(0, parts - 1, start, 0)
+
+    def own_sum(half):
+        return pltpu.make_async_copy(sum_buf.at[half], full_buf.at[half, mine], own_sem.at[6 + half])
+
+    def add_parts(half):
+        wait_bytes(part_buf.at[half, pl.ds(0, parts - 1)], red_recv.at[half])
+        own_part(half).wait()
+        total = part_buf[half, 0].astype(F32)
+        for part in range(1, parts):
+            total = total + part_buf[half, part].astype(F32)
+        sum_buf[half] = total.astype(BF16)
+        start_sum(half)
+        own_sum(half).start()
+
+    for half in range(2):
+        if half == 1:
+            add_parts(0)
         wait_bytes(others(recv_buf, half), recv_sem.at[half])
         own_copy(half).wait()
         rows = jnp.concatenate(
@@ -176,45 +237,18 @@
         ret_send[half, 1] = result[:, COLS:].reshape(blocks, ROWS, COLS)
         send_back(half)
         own_back(half).start()
-        cross_rows[half] = inverse_inner(gate_re * grad_re + gate_im * grad_im, gate_re * grad_im - gate_im * grad_re)
-
-    cross = dot(outer_inv[...], jnp.concatenate([cross_rows[0], cross_rows[1]], axis=1)).astype(BF16)
-    for half in range(2):
-        cross_buf[:, half * ROWS:(half + 1) * ROWS] = cross[:, half * COLS:(half + 1) * COLS].reshape(blocks, ROWS, COLS)
-
-    def start_part(step, carry):
-        dest = (mine + 1 + step) % parts
-        pltpu.make_async_remote_copy(
-            src_ref=cross_buf.at[pl.ds(dest * piece, piece)], dst_ref=part_buf.at[mine],
-            send_sem=red_send.at[0], recv_sem=red_recv.at[0], device_id={"dp": dest}, device_id_type=MESH,
-        ).start()
-        return carry
-
-    lax.fori_loop(0, parts - 1, start_part, 0)
-    own_part = pltpu.make_async_copy(cross_buf.at[pl.ds(mine * piece, piece)], part_buf.at[mine], own_sem.at[4])
-    own_part.start()
-    wait_bytes(part_buf.at[pl.ds(0, parts - 1)], red_recv.at[0])
-    own_part.wait()
-    total = part_buf[0].astype(F32)
-    for part in range(1, parts):
-        total = total + part_buf[part].astype(F32)
-    sum_buf[...] = total.astype(BF16)
-
-    def start_sum(step, carry):
-        dest = (mine + 1 + step) % parts
-        pltpu.make_async_remote_copy(
-            src_ref=sum_buf, dst_ref=full_buf.at[mine],
-            send_sem=all_send.at[0], recv_sem=all_recv.at[0], device_id={"dp": dest}, device_id_type=MESH,
-        ).start()
-        return carry
-
-    lax.fori_loop(0, parts - 1, start_sum, 0)
-    own_sum = pltpu.make_async_copy(sum_buf, full_buf.at[mine], own_sem.at[5])
-    own_sum.start()
-    wait_bytes(full_buf.at[pl.ds(0, parts - 1)], all_recv.at[0])
-    own_sum.wait()
-    for a in range(blocks):
-        filt_out[:, a * COLS:(a + 1) * COLS] = full_buf[a // piece, a % piece].astype(filt_out.dtype)
+        cross = inverse_inner(gate_re * grad_re + gate_im * grad_im, gate_re * grad_im - gate_im * grad_re)
+        cross_buf[half] = dot(outer_inv[...], cross).astype(BF16).reshape(blocks, ROWS, COLS)
+        start_part(half)
+        own_part(half).start()
+
+    add_parts(1)
+    for half in range(2):
+        wait_bytes(full_buf.at[half, pl.ds(0, parts - 1)], all_recv.at[half])
+        own_sum(half).wait()
+        for a in range(blocks):
+            lanes = slice(a * COLS, (a + 1) * COLS)
+            filt_out[half * ROWS:(half + 1) * ROWS, lanes] = full_buf[half, a // piece, a % piece]
 
     for half in range(2):
         wait_bytes(others(ret_recv, half), ret_recv_sem.at[half])
@@ -228,8 +262,8 @@
     for half in range(2):
         wait_bytes(others(send_buf, half), send_sem.at[half])
         wait_bytes(others(ret_send, half), ret_send_sem.at[half])
-    wait_bytes(part_buf.at[pl.ds(0, parts - 1)], red_send.at[0])
-    wait_bytes(full_buf.at[pl.ds(0, parts - 1)], all_send.at[0])
+        wait_bytes(part_buf.at[half, pl.ds(0, parts - 1)], red_send.at[half])
+        wait_bytes(full_buf.at[half, pl.ds(0, parts - 1)], all_send.at[half])
 
 
 def local(blocks, parts, cols, query_proj, key_proj, value_proj, out_grad, filter_taps):
@@ -239,6 +273,9 @@
     piece = blocks // parts
     messages = (2, 2, blocks, ROWS, COLS)
     vmem = pl.BlockSpec(memory_space=pltpu.VMEM)
+    hbm = pl.BlockSpec(memory_space=pltpu.HBM)
+    operands = (query_proj[0], key_proj[0], value_proj[0], out_grad[0], filter_taps, *map(jnp.asarray, tables))
+    operands = tuple(pltpu.with_memory_space_constraint(operand, pltpu.HBM) for operand in operands)
     conv_local, back_local, filt_sum = pl.pallas_call(
         functools.partial(kernel, blocks, parts, cols),
         out_shape=(
@@ -246,34 +283,35 @@
             jax.ShapeDtypeStruct((tokens, channels), BF16),
             jax.ShapeDtypeStruct(filter_taps.shape, BF16),
         ),
-        in_specs=[vmem] * 11,
+        in_specs=[hbm] * 11,
         out_specs=(vmem,) * 3,
         scratch_shapes=[
+            *(pltpu.VMEM(operand.shape, operand.dtype) for operand in operands),
             pltpu.VMEM(messages, BF16),
             pltpu.VMEM(messages, BF16),
             pltpu.VMEM(messages, BF16),
             pltpu.VMEM(messages, BF16),
             pltpu.VMEM((2, span, COLS), F32),
             pltpu.VMEM((2, span, COLS), F32),
-            pltpu.VMEM((2, 2 * span, COLS), BF16),
-            pltpu.VMEM((blocks, 2 * ROWS, COLS), BF16),
-            pltpu.VMEM((parts, piece, 2 * ROWS, COLS), BF16),
-            pltpu.VMEM((piece, 2 * ROWS, COLS), BF16),
-            pltpu.VMEM((parts, piece, 2 * ROWS, COLS), BF16),
-            pltpu.SemaphoreType.DMA((2,)),
-            pltpu.SemaphoreType.DMA((2,)),
-            pltpu.SemaphoreType.DMA((2,)),
-            pltpu.SemaphoreType.DMA((2,)),
-            pltpu.SemaphoreType.DMA((6,)),
-            pltpu.SemaphoreType.DMA((1,)),
-            pltpu.SemaphoreType.DMA((1,)),
-            pltpu.SemaphoreType.DMA((1,)),
-            pltpu.SemaphoreType.DMA((1,)),
+            pltpu.VMEM((2, blocks, ROWS, COLS), BF16),
+            pltpu.VMEM((2, parts, piece, ROWS, COLS), BF16),
+            pltpu.VMEM((2, piece, ROWS, COLS), BF16),
+            pltpu.VMEM((2, parts, piece, ROWS, COLS), BF16),
+            pltpu.SemaphoreType.DMA((2,)),
+            pltpu.SemaphoreType.DMA((2,)),
+            pltpu.SemaphoreType.DMA((2,)),
+            pltpu.SemaphoreType.DMA((2,)),
+            pltpu.SemaphoreType.DMA((8,)),
+            pltpu.SemaphoreType.DMA((11,)),
+            pltpu.SemaphoreType.DMA((2,)),
+            pltpu.SemaphoreType.DMA((2,)),
+            pltpu.SemaphoreType.DMA((2,)),
+            pltpu.SemaphoreType.DMA((2,)),
         ],
         compiler_params=pltpu.CompilerParams(
-            collective_id=0, has_side_effects=True, vmem_limit_bytes=56 * 2**20
+            collective_id=0, has_side_effects=True, vmem_limit_bytes=24 * 2**20
         ),
-    )(query_proj[0], key_proj[0], value_proj[0], out_grad[0], filter_taps, *map(jnp.asarray, tables))
+    )(*operands)
     back_vals = back_local.astype(F32)
     grad_q = (back_vals * key_proj[0].astype(F32)).astype(BF16)[None]
     grad_k = (back_vals * query_proj[0].astype(F32)).astype(BF16)[None]

time: 71.1 us -> 66.8 us (0.940)
  the two profiles are of different devices: /device:TPU:353 before, /device:TPU:260 now
where the time goes in v2:
time: 66.8 us; the launch traced here: 66.7 us
  Pallas kernels  64.1 us (96%)
  other arithmetic  1.88 us (3%)
  between operations  0.69 us (1%)
    pallas_call x1, Pallas kernels, local(): pl.pallas_call(functools.partial(kernel, blocks, parts, cols), out_shape=...  64.1 us

profile of v2, /device:TPU:260, one launch (start us, length us, event | category | flops | bytes accessed | tf_op | source)
XLA Modules:
  0.0 66.7 jit_solution(10372828105108549727)
XLA Ops:
  0.6 0.0 copy-start
  0.6 0.0 copy-start.1
  0.7 0.0 copy-start.2
  0.7 64.1 %shard_map.138 = (bf16[128,1024]{1,0:T(8,128)(2,1)S(1)}, bf16[128,1024]{1,0:T(8,128)(2,1)S(1)}, bf16[32,4096]{1,0:T(8,128)(2,1)S(1)}) custom-call(bf16[128,1024]{1,0:T(8,128)(2,1)} %bitcast.13, bf16[128,1024]{1,0:T(8,128)(2,1)} %bitcast.14, bf16[128,1024]{1,0:T(8,128)(2,1)} %bitcast.16, bf16[128,1024]{1,0:T(8,128)(2,1)} %bitcast.15, f32[32,4096]{1,0:T(8,128)} %taps_hbm.1, ...), custom_call_target="tpu_custom_call" | custom-call | tf_op jit(solution)/shard_map/pallas_call | solution.py:279
  64.8 0.0 copy-done
  64.8 0.0 copy-done.1
  64.8 0.0 copy-done.2
  64.8 1.1 %fusion.3 = (bf16[1,128,1024]{2,1,0:T(8,128)(2,1)}, bf16[1,128,1024]{2,1,0:T(8,128)(2,1)}, bf16[1,128,1024]{2,1,0:T(8,128)(2,1)}) fusion(bf16[128,1024]{1,0:T(8,128)(2,1)S(1)} %get-tuple-element.7, bf16[1,128,1024]{2,1,0:T(8,128)(2,1)S(1)} %copy-done, bf16[1,128,1024]{2,1,0:T(8,128)(2,1)S(1)} %copy-done.1, bf16[128,1024]{1,0:T(8,128)(2,1)S(1)} %get-tuple-element.8, ...), kind=kLoop, calls=%fused_computation.6 | loop fusion | flops 1441792 | bytes 2097152 | tf_op jit(solution)/shard_map/broadcast_in_dim | solution.py:317
  65.9 0.8 %convert_element_type.35 = f32[32,4096]{1,0:T(8,128)} convert(bf16[32,4096]{1,0:T(8,128)(2,1)S(1)} %get-tuple-element.9) | non-fusion elementwise | flops 131072 | bytes 786432 | tf_op jit(solution)/shard_map/convert_element_type | solution.py:319
Async XLA Ops:
  0.6 64.2 %copy-start = (bf16[1,128,1024]{2,1,0:T(8,128)(2,1)S(1)}, bf16[1,128,1024]{2,1,0:T(8,128)(2,1)}, u32[]{:S(2)}) copy-start(bf16[1,128,1024]{2,1,0:T(8,128)(2,1)} %param.11) | copy-start | bytes 786436
  0.6 64.2 %copy-start.1 = (bf16[1,128,1024]{2,1,0:T(8,128)(2,1)S(1)}, bf16[1,128,1024]{2,1,0:T(8,128)(2,1)}, u32[]{:S(2)}) copy-start(bf16[1,128,1024]{2,1,0:T(8,128)(2,1)} %param.12) | copy-start | bytes 786436
  0.7 64.2 %copy-start.2 = (bf16[1,128,1024]{2,1,0:T(8,128)(2,1)S(1)}, bf16[1,128,1024]{2,1,0:T(8,128)(2,1)}, u32[]{:S(2)}) copy-start(bf16[1,128,1024]{2,1,0:T(8,128)(2,1)} %param.14) | copy-start | bytes 786436

commit v3 on v2

--- a/solution.py
+++ b/solution.py
@@ -54,29 +54,34 @@
     me = lax.axis_index("ctx")
     mine = lax.axis_index("dp")
     lines = blocks // cols
-    row_at, col_at = me // cols, me % cols
+    row_at, col_at = lax.div(me, cols), lax.rem(me, cols)
     span = blocks * ROWS
     group = COLS // (2 * ROWS)
     piece = blocks // parts
 
-    def peer(step):
-        turn = step // lines
-        shift = cols // 2 + ((turn + 1) // 2) * (1 - 2 * (turn % 2))
-        down = (step % lines + 1) % lines
-        return ((row_at + down) % lines) * cols + (col_at + shift) % cols
+    line_starts = [lax.rem(row_at + down, lines) * cols for down in range(1, lines + 1)]
+
+    def for_peers(act, first=0, last=cols):
+        def turn(step, carry):
+            odd = lax.rem(step, 2)
+            shift = cols // 2 + lax.div(step + 1, 2) * (1 - 2 * odd)
+            column = lax.rem(col_at + shift, cols)
+            for start in line_starts:
+                act(start + column)
+            return carry
+
+        lax.fori_loop(first, min(last, cols - 1), turn, 0)
+        if last == cols:
+            for start in line_starts[:-1]:
+                act(start + col_at)
+
+    def for_parts(act):
+        for step in range(1, parts):
+            act(lax.rem(mine + step, parts))
 
     barrier = pltpu.get_barrier_semaphore()
-
-    def greet(step, carry):
-        pl.semaphore_signal(barrier, inc=1, device_id={"ctx": peer(step)}, device_id_type=MESH)
-        return carry
-
-    def greet_part(step, carry):
-        pl.semaphore_signal(barrier, inc=1, device_id={"dp": (mine + 1 + step) % parts}, device_id_type=MESH)
-        return carry
-
-    lax.fori_loop(0, blocks - 1, greet, 0)
-    lax.fori_loop(0, parts - 1, greet_part, 0)
+    for_peers(lambda dest: pl.semaphore_signal(barrier, inc=1, device_id={"ctx": dest}, device_id_type=MESH))
+    for_parts(lambda dest: pl.semaphore_signal(barrier, inc=1, device_id={"dp": dest}, device_id_type=MESH))
 
     loads = [
         pltpu.make_async_copy(source, target, load_sem.at[number])
@@ -104,34 +109,30 @@
     pl.semaphore_wait(barrier, blocks - 1 + parts - 1)
 
     def send_tokens(half):
-        def start(step, carry):
-            dest = peer(step)
+        def start(dest):
             pltpu.make_async_remote_copy(
                 src_ref=send_buf.at[half, :, dest], dst_ref=recv_buf.at[half, :, me],
                 send_sem=send_sem.at[half], recv_sem=recv_sem.at[half],
                 device_id={"ctx": dest}, device_id_type=MESH,
             ).start()
-            return carry
-
-        lax.fori_loop(0, blocks - 1, start, 0)
-
-    def send_back(half):
-        def start(step, carry):
-            dest = peer(step)
+
+        for_peers(start)
+
+    def send_back(first, last):
+        def start(dest):
             pltpu.make_async_remote_copy(
-                src_ref=ret_send.at[half, :, dest], dst_ref=ret_recv.at[half, :, me],
-                send_sem=ret_send_sem.at[half], recv_sem=ret_recv_sem.at[half],
+                src_ref=ret_send.at[:, :, dest], dst_ref=ret_recv.at[:, :, me],
+                send_sem=ret_send_sem.at[0], recv_sem=ret_recv_sem.at[0],
                 device_id={"ctx": dest}, device_id_type=MESH,
             ).start()
-            return carry
-
-        lax.fori_loop(0, blocks - 1, start, 0)
+
+        for_peers(start, first, last)
 
     def wait_bytes(ref, sem):
         pltpu.make_async_copy(ref, ref, sem).wait()
 
-    def others(ref, half):
-        return ref.at[half, :, pl.ds(0, blocks - 1)]
+    def others(ref):
+        return ref.at[:, :, pl.ds(0, blocks - 1)]
 
     def own_copy(half):
         return pltpu.make_async_copy(send_buf.at[half, :, me], recv_buf.at[half, :, me], own_sem.at[half])
@@ -181,15 +182,13 @@
         filt_im[half] = imag
 
     def start_part(half):
-        def start(step, carry):
-            dest = (mine + 1 + step) % parts
+        def start(dest):
             pltpu.make_async_remote_copy(
                 src_ref=cross_buf.at[half, pl.ds(dest * piece, piece)], dst_ref=part_buf.at[half, mine],
                 send_sem=red_send.at[half], recv_sem=red_recv.at[half], device_id={"dp": dest}, device_id_type=MESH,
             ).start()
-            return carry
-
-        lax.fori_loop(0, parts - 1, start, 0)
+
+        for_parts(start)
 
     def own_part(half):
         return pltpu.make_async_copy(
@@ -197,15 +196,13 @@
         )
 
     def start_sum(half):
-        def start(step, carry):
-            dest = (mine + 1 + step) % parts
+        def start(dest):
             pltpu.make_async_remote_copy(
                 src_ref=sum_buf.at[half], dst_ref=full_buf.at[half, mine],
                 send_sem=all_send.at[half], recv_sem=all_recv.at[half], device_id={"dp": dest}, device_id_type=MESH,
             ).start()
-            return carry
-
-        lax.fori_loop(0, parts - 1, start, 0)
+
+        for_parts(start)
 
     def own_sum(half):
         return pltpu.make_async_copy(sum_buf.at[half], full_buf.at[half, mine], own_sem.at[6 + half])
@@ -221,28 +218,27 @@
         own_sum(half).start()
 
     for half in range(2):
-        if half == 1:
-            add_parts(0)
-        wait_bytes(others(recv_buf, half), recv_sem.at[half])
+        wait_bytes(recv_buf.at[half, :, pl.ds(0, blocks - 1)], recv_sem.at[half])
         own_copy(half).wait()
         rows = jnp.concatenate(
             [recv_buf[half, 0].reshape(span, COLS), recv_buf[half, 1].reshape(span, COLS)], axis=1
         )
         (gate_re, gate_im), (grad_re, grad_im) = forward(rows)
+        cross = inverse_inner(gate_re * grad_re + gate_im * grad_im, gate_re * grad_im - gate_im * grad_re)
+        cross_buf[half] = dot(outer_inv[...], cross).astype(BF16).reshape(blocks, ROWS, COLS)
+        start_part(half)
+        own_part(half).start()
         tap_re, tap_im = filt_re[half], filt_im[half]
         conv = inverse_inner(gate_re * tap_re - gate_im * tap_im, gate_re * tap_im + gate_im * tap_re)
         back = inverse_inner(grad_re * tap_re + grad_im * tap_im, grad_im * tap_re - grad_re * tap_im)
         result = dot(outer_inv[...], jnp.concatenate([conv, back], axis=1)).astype(BF16)
         ret_send[half, 0] = result[:, :COLS].reshape(blocks, ROWS, COLS)
         ret_send[half, 1] = result[:, COLS:].reshape(blocks, ROWS, COLS)
-        send_back(half)
         own_back(half).start()
-        cross = inverse_inner(gate_re * grad_re + gate_im * grad_im, gate_re * grad_im - gate_im * grad_re)
-        cross_buf[half] = dot(outer_inv[...], cross).astype(BF16).reshape(blocks, ROWS, COLS)
-        start_part(half)
-        own_part(half).start()
-
-    add_parts(1)
+
+    send_back(0, cols)
+    for half in range(2):
+        add_parts(half)
     for half in range(2):
         wait_bytes(full_buf.at[half, pl.ds(0, parts - 1)], all_recv.at[half])
         own_sum(half).wait()
@@ -250,8 +246,8 @@
             lanes = slice(a * COLS, (a + 1) * COLS)
             filt_out[half * ROWS:(half + 1) * ROWS, lanes] = full_buf[half, a // piece, a % piece]
 
-    for half in range(2):
-        wait_bytes(others(ret_recv, half), ret_recv_sem.at[half])
+    wait_bytes(others(ret_recv), ret_recv_sem.at[0])
+    for half in range(2):
         own_back(half).wait()
     for number, out_ref in enumerate((conv_out, back_out)):
         for block in range(blocks // group):
@@ -260,10 +256,27 @@
             out_ref[:, block * COLS:(block + 1) * COLS] = rows.reshape(COLS, COLS).astype(F32).T.astype(BF16)
 
     for half in range(2):
-        wait_bytes(others(send_buf, half), send_sem.at[half])
-        wait_bytes(others(ret_send, half), ret_send_sem.at[half])
+        wait_bytes(send_buf.at[half, :, pl.ds(0, blocks - 1)], send_sem.at[half])
+    wait_bytes(others(ret_send), ret_send_sem.at[0])
+    for half in range(2):
         wait_bytes(part_buf.at[half, pl.ds(0, parts - 1)], red_send.at[half])
         wait_bytes(full_buf.at[half, pl.ds(0, parts - 1)], all_send.at[half])
+
+
+def finish(conv_ref, back_ref, query_ref, key_ref, grad_ref, filt_ref, *rest):
+    outs, bufs, sem = rest[:4], rest[4:8], rest[8]
+    copies = [pltpu.make_async_copy(buf, out, sem.at[number]) for number, (buf, out) in enumerate(zip(bufs, outs))]
+    bufs[3][...] = filt_ref[...].astype(F32)
+    copies[3].start()
+    back_vals = back_ref[...].astype(F32)
+    bufs[0][...] = (back_vals * key_ref[...].astype(F32)).astype(BF16)
+    copies[0].start()
+    bufs[1][...] = (back_vals * query_ref[...].astype(F32)).astype(BF16)
+    copies[1].start()
+    bufs[2][...] = (grad_ref[...].astype(F32) * conv_ref[...].astype(F32)).astype(BF16)
+    copies[2].start()
+    for copy in copies:
+        copy.wait()
 
 
 def local(blocks, parts, cols, query_proj, key_proj, value_proj, out_grad, filter_taps):
@@ -312,11 +325,20 @@
             collective_id=0, has_side_effects=True, vmem_limit_bytes=24 * 2**20
         ),
     )(*operands)
-    back_vals = back_local.astype(F32)
-    grad_q = (back_vals * key_proj[0].astype(F32)).astype(BF16)[None]
-    grad_k = (back_vals * query_proj[0].astype(F32)).astype(BF16)[None]
-    grad_v = (out_grad[0].astype(F32) * conv_local.astype(F32)).astype(BF16)[None]
-    return grad_q, grad_k, grad_v, filt_sum.astype(F32)
+    outs = ((tokens, channels), (tokens, channels), (tokens, channels), filter_taps.shape)
+    kinds = (BF16, BF16, BF16, F32)
+    grad_q, grad_k, grad_v, grad_filt = pl.pallas_call(
+        finish,
+        out_shape=tuple(jax.ShapeDtypeStruct(shape, kind) for shape, kind in zip(outs, kinds)),
+        in_specs=[vmem] * 6,
+        out_specs=(pl.BlockSpec(memory_space=pl.ANY),) * 4,
+        scratch_shapes=[
+            *(pltpu.VMEM(shape, kind) for shape, kind in zip(outs, kinds)),
+            pltpu.SemaphoreType.DMA((4,)),
+        ],
+        compiler_params=pltpu.CompilerParams(vmem_limit_bytes=8 * 2**20),
+    )(conv_local, back_local, query_proj[0], key_proj[0], out_grad[0], filt_sum)
+    return grad_q[None], grad_k[None], grad_v[None], grad_filt
 
 
 def solution(mesh):

time: 66.8 us -> 63.7 us (0.954)
  the two profiles are of different devices: /device:TPU:260 before, /device:TPU:384 now
where the time goes in v3:
time: 63.7 us; the launch traced here: 63.6 us
  Pallas kernels  62.9 us (99%)
  between operations  0.69 us (1%)
    pallas_call x1, Pallas kernels, local(): pl.pallas_call(functools.partial(kernel, blocks, parts, cols), out_shape=...  61.7 us

profile of v3, /device:TPU:384, one launch (start us, length us, event | category | flops | bytes accessed | tf_op | source)
XLA Modules:
  0.0 63.6 jit_solution(17834801526615550067)
XLA Ops:
  0.6 0.0 copy-start
  0.6 0.0 copy-start.1
  0.7 0.0 copy-start.2
  0.7 61.7 %shard_map.138 = (bf16[128,1024]{1,0:T(8,128)(2,1)S(1)}, bf16[128,1024]{1,0:T(8,128)(2,1)S(1)}, bf16[32,4096]{1,0:T(8,128)(2,1)S(1)}) custom-call(bf16[128,1024]{1,0:T(8,128)(2,1)} %bitcast.7, bf16[128,1024]{1,0:T(8,128)(2,1)} %bitcast.9, bf16[128,1024]{1,0:T(8,128)(2,1)} %bitcast.13, bf16[128,1024]{1,0:T(8,128)(2,1)} %bitcast.11, f32[32,4096]{1,0:T(8,128)} %taps_hbm.1, ...), custom_call_target="tpu_custom_call" | custom-call | tf_op jit(solution)/shard_map/pallas_call | solution.py:292
  62.4 0.0 copy-done
  62.4 0.0 copy-done.1
  62.4 0.0 copy-done.2
  62.4 1.1 %shard_map.139 = (bf16[128,1024]{1,0:T(8,128)(2,1)}, bf16[128,1024]{1,0:T(8,128)(2,1)}, bf16[128,1024]{1,0:T(8,128)(2,1)}, f32[32,4096]{1,0:T(8,128)}) custom-call(bf16[128,1024]{1,0:T(8,128)(2,1)S(1)} %get-tuple-element.11.conv_ref, bf16[128,1024]{1,0:T(8,128)(2,1)S(1)} %get-tuple-element.12.back_ref, bf16[128,1024]{1,0:T(8,128)(2,1)S(1)} %bitcast.8, ...), custom_call_target="tpu_custom_call" | custom-call | tf_op jit(solution)/shard_map/pallas_call | solution.py:330
Async XLA Ops:
  0.6 61.8 %copy-start = (bf16[1,128,1024]{2,1,0:T(8,128)(2,1)S(1)}, bf16[1,128,1024]{2,1,0:T(8,128)(2,1)}, u32[]{:S(2)}) copy-start(bf16[1,128,1024]{2,1,0:T(8,128)(2,1)} %param.11) | copy-start | bytes 786436
  0.6 61.8 %copy-start.1 = (bf16[1,128,1024]{2,1,0:T(8,128)(2,1)S(1)}, bf16[1,128,1024]{2,1,0:T(8,128)(2,1)}, u32[]{:S(2)}) copy-start(bf16[1,128,1024]{2,1,0:T(8,128)(2,1)} %param.12) | copy-start | bytes 786436
  0.7 61.8 %copy-start.2 = (bf16[1,128,1024]{2,1,0:T(8,128)(2,1)S(1)}, bf16[1,128,1024]{2,1,0:T(8,128)(2,1)}, u32[]{:S(2)}) copy-start(bf16[1,128,1024]{2,1,0:T(8,128)(2,1)} %param.14) | copy-start | bytes 786436

commit v4 on v3

--- a/solution.py
+++ b/solution.py
@@ -71,7 +71,7 @@
             return carry
 
         lax.fori_loop(first, min(last, cols - 1), turn, 0)
-        if last == cols:
+        if first < last == cols:
             for start in line_starts[:-1]:
                 act(start + col_at)
 
@@ -224,10 +224,11 @@
             [recv_buf[half, 0].reshape(span, COLS), recv_buf[half, 1].reshape(span, COLS)], axis=1
         )
         (gate_re, gate_im), (grad_re, grad_im) = forward(rows)
-        cross = inverse_inner(gate_re * grad_re + gate_im * grad_im, gate_re * grad_im - gate_im * grad_re)
-        cross_buf[half] = dot(outer_inv[...], cross).astype(BF16).reshape(blocks, ROWS, COLS)
-        start_part(half)
-        own_part(half).start()
+        if half == 0:
+            cross = inverse_inner(gate_re * grad_re + gate_im * grad_im, gate_re * grad_im - gate_im * grad_re)
+            cross_buf[half] = dot(outer_inv[...], cross).astype(BF16).reshape(blocks, ROWS, COLS)
+            start_part(half)
+            own_part(half).start()
         tap_re, tap_im = filt_re[half], filt_im[half]
         conv = inverse_inner(gate_re * tap_re - gate_im * tap_im, gate_re * tap_im + gate_im * tap_re)
         back = inverse_inner(grad_re * tap_re + grad_im * tap_im, grad_im * tap_re - grad_re * tap_im)
@@ -235,8 +236,14 @@
         ret_send[half, 0] = result[:, :COLS].reshape(blocks, ROWS, COLS)
         ret_send[half, 1] = result[:, COLS:].reshape(blocks, ROWS, COLS)
         own_back(half).start()
-
-    send_back(0, cols)
+        if half == 1:
+            send_back(0, 1)
+            cross = inverse_inner(gate_re * grad_re + gate_im * grad_im, gate_re * grad_im - gate_im * grad_re)
+            cross_buf[half] = dot(outer_inv[...], cross).astype(BF16).reshape(blocks, ROWS, COLS)
+            start_part(half)
+            own_part(half).start()
+
+    send_back(1, cols)
     for half in range(2):
         add_parts(half)
     for half in range(2):

time: 63.7 us -> 62.6 us (0.983)
  the two profiles are of different devices: /device:TPU:384 before, /device:TPU:390 now
where the time goes in v4:
time: 62.6 us; the launch traced here: 62.5 us
  Pallas kernels  61.8 us (99%)
  between operations  0.69 us (1%)
    pallas_call x1, Pallas kernels, local(): pl.pallas_call(functools.partial(kernel, blocks, parts, cols), out_shape=...  60.7 us

profile of v4, /device:TPU:390, one launch (start us, length us, event | category | flops | bytes accessed | tf_op | source)
XLA Modules:
  0.0 62.5 jit_solution(3594589989670307268)
XLA Ops:
  0.6 0.0 copy-start
  0.6 0.0 copy-start.1
  0.7 0.0 copy-start.2
  0.7 60.7 %shard_map.138 = (bf16[128,1024]{1,0:T(8,128)(2,1)S(1)}, bf16[128,1024]{1,0:T(8,128)(2,1)S(1)}, bf16[32,4096]{1,0:T(8,128)(2,1)S(1)}) custom-call(bf16[128,1024]{1,0:T(8,128)(2,1)} %bitcast.7, bf16[128,1024]{1,0:T(8,128)(2,1)} %bitcast.9, bf16[128,1024]{1,0:T(8,128)(2,1)} %bitcast.13, bf16[128,1024]{1,0:T(8,128)(2,1)} %bitcast.11, f32[32,4096]{1,0:T(8,128)} %taps_hbm.1, ...), custom_call_target="tpu_custom_call" | custom-call | tf_op jit(solution)/shard_map/pallas_call | solution.py:299
  61.3 0.0 copy-done
  61.3 0.0 copy-done.1
  61.3 0.0 copy-done.2
  61.4 1.1 %shard_map.139 = (bf16[128,1024]{1,0:T(8,128)(2,1)}, bf16[128,1024]{1,0:T(8,128)(2,1)}, bf16[128,1024]{1,0:T(8,128)(2,1)}, f32[32,4096]{1,0:T(8,128)}) custom-call(bf16[128,1024]{1,0:T(8,128)(2,1)S(1)} %get-tuple-element.11.conv_ref, bf16[128,1024]{1,0:T(8,128)(2,1)S(1)} %get-tuple-element.12.back_ref, bf16[128,1024]{1,0:T(8,128)(2,1)S(1)} %bitcast.8, ...), custom_call_target="tpu_custom_call" | custom-call | tf_op jit(solution)/shard_map/pallas_call | solution.py:337
Async XLA Ops:
  0.6 60.7 %copy-start = (bf16[1,128,1024]{2,1,0:T(8,128)(2,1)S(1)}, bf16[1,128,1024]{2,1,0:T(8,128)(2,1)}, u32[]{:S(2)}) copy-start(bf16[1,128,1024]{2,1,0:T(8,128)(2,1)} %param.11) | copy-start | bytes 786436
  0.6 60.7 %copy-start.1 = (bf16[1,128,1024]{2,1,0:T(8,128)(2,1)S(1)}, bf16[1,128,1024]{2,1,0:T(8,128)(2,1)}, u32[]{:S(2)}) copy-start(bf16[1,128,1024]{2,1,0:T(8,128)(2,1)} %param.12) | copy-start | bytes 786436
  0.7 60.7 %copy-start.2 = (bf16[1,128,1024]{2,1,0:T(8,128)(2,1)S(1)}, bf16[1,128,1024]{2,1,0:T(8,128)(2,1)}, u32[]{:S(2)}) copy-start(bf16[1,128,1024]{2,1,0:T(8,128)(2,1)} %param.14) | copy-start | bytes 786436
